TPU v7x, 32 devices: a whole 2x2x4 slice. The times are simulated.
32 devices in a mesh: batch: 4 (over y, x), ctx: 8 (over z, core).
Axes of the slice: x: 2, y: 2, z: 4, core: 2. Of those that a mesh axis runs over, the one named last changes fastest.
Arguments:
- hidden: bfloat16 [4, 1024, 768], P('batch', 'ctx'), may hold values from -6 to 6
- cotangent: bfloat16 [4, 1024, 768], P('batch', 'ctx'), may hold values from -6 to 6
- w_qkv: bfloat16 [768, 2304], P(('batch', 'ctx')), may hold values from -3 to 3
- w_proj: bfloat16 [768, 768], P(('batch', 'ctx')), may hold values from -1.25 to 1.25
- w_inner: bfloat16 [768, 2304], P(('batch', 'ctx')), may hold values from -0.21875 to 0.21875
- w_down: bfloat16 [768, 1152], P(('batch', 'ctx')), may hold values from -0.1875 to 0.1875
- norm1_gain: bfloat16 [768], P(('batch', 'ctx')), may hold values from 0.5 to 1.5
- norm2_gain: bfloat16 [768], P(('batch', 'ctx')), may hold values from 0.5 to 1.5
Outputs:
- hidden_out: bfloat16 [4, 1024, 768], P('batch', 'ctx')
- hidden_grad: float32 [4, 1024, 768], P('batch', 'ctx')
- qkv_grad: float32 [768, 2304], P(('batch', 'ctx'))
- proj_grad: float32 [768, 768], P(('batch', 'ctx'))
- inner_grad: float32 [768, 2304], P(('batch', 'ctx'))
- down_grad: float32 [768, 1152], P(('batch', 'ctx'))
- norm1_grad: float32 [768], P(('batch', 'ctx'))
- norm2_grad: float32 [768], P(('batch', 'ctx'))
All inputs are finite; a program needn't handle non-finite values.
Results may differ from a plain program's by a relative error of at most 0.02.
Values may be sent and summed in bfloat16 or wider, within the bound.
A program may use at most 192 MiB of HBM per device.

v0:
```python
import jax
import jax.numpy as jnp
from jax import lax
from jax.sharding import PartitionSpec as P

D = 768
HEADS = 12
HEAD_DIM = 64
FF = 1152
norm_eps = 1e-05
rope_base = 160000.0


def apply_layer_norm(values, gain_vector):
    centre = jnp.mean(values, axis=-1, keepdims=True)
    shifted = values - centre
    spread = jnp.mean(shifted * shifted, axis=-1, keepdims=True)
    inverse = lax.rsqrt(spread + norm_eps)
    normed = shifted * inverse
    return (normed * gain_vector, normed, inverse)


def layer_norm_gradient(upstream, gain_vector, normed, inverse):
    scaled = upstream * gain_vector
    first_mean = jnp.mean(scaled, axis=-1, keepdims=True)
    second_mean = jnp.mean(scaled * normed, axis=-1, keepdims=True)
    return (
        inverse * (scaled - first_mean - normed * second_mean),
        jnp.sum(upstream * normed, axis=0),
    )


def rope_tables(offset, row_count, head_width):
    half_dim = head_width // 2
    position = (offset + jnp.arange(row_count, dtype=jnp.int32)).astype(jnp.float32)
    exponent = jnp.arange(half_dim, dtype=jnp.int32).astype(jnp.float32) * (-2.0 / head_width)
    angles = position[:, None] * jnp.power(rope_base, exponent)[None, :]
    return (jnp.cos(angles), jnp.sin(angles))


def rotate(values, cosine, sine_table, direction):
    half_dim = values.shape[-1] // 2
    front_half = values[..., :half_dim]
    back_half = values[..., half_dim:]
    cos_rows = cosine[:, None, :]
    sin_rows = sine_table[:, None, :] * direction
    return jnp.concatenate(
        [
            front_half * cos_rows - back_half * sin_rows,
            back_half * cos_rows + front_half * sin_rows,
        ],
        axis=-1,
    )


def gelu_parts(act_input):
    normal_cdf = 0.5 * (1.0 + jax.scipy.special.erf(act_input * 0.7071067811865476))
    density = jnp.exp(-0.5 * act_input * act_input) * 0.3989422804014327
    return (act_input * normal_cdf, normal_cdf + act_input * density)


def as_heads(flat_rows):
    return flat_rows.reshape(flat_rows.shape[0], HEADS, HEAD_DIM)


def pair_terms(query_rows, grad_rows, log_rows, delta_rows, key_rows, value_rows, score_scale):
    scores = (
        jnp.einsum("qhd,khd->hqk", query_rows, key_rows, preferred_element_type=jnp.float32)
        * score_scale
    )
    probabilities = jnp.exp(scores - log_rows[..., None])
    grad_dots = jnp.einsum(
        "qhd,khd->hqk", grad_rows, value_rows, preferred_element_type=jnp.float32
    )
    dscore = (probabilities * (grad_dots - delta_rows[..., None])).astype(jnp.bfloat16)
    return (probabilities.astype(jnp.bfloat16), dscore)


def local(hidden, cotangent, w_qkv, w_proj, w_inner, w_down, norm1_gain, norm2_gain):
    token_rows = hidden.shape[1]
    score_scale = HEAD_DIM ** (-0.5)
    full_qkv, full_proj, full_inner, full_down, gain_first, gain_second = (
        lax.all_gather(w_qkv, ("batch", "ctx"), axis=0, tiled=True),
        lax.all_gather(w_proj, ("batch", "ctx"), axis=0, tiled=True),
        lax.all_gather(w_inner, ("batch", "ctx"), axis=0, tiled=True),
        lax.all_gather(w_down, ("batch", "ctx"), axis=0, tiled=True),
        lax.all_gather(norm1_gain, ("batch", "ctx"), axis=0, tiled=True),
        lax.all_gather(norm2_gain, ("batch", "ctx"), axis=0, tiled=True),
    )
    first_norm_gain = gain_first.astype(jnp.float32)
    second_norm_gain = gain_second.astype(jnp.float32)
    input_tokens = hidden[0].astype(jnp.float32)
    first_normed_rows, first_centered_rows, first_inverse_deviation = apply_layer_norm(
        input_tokens, first_norm_gain
    )
    h_one = first_normed_rows.astype(jnp.bfloat16)
    projected = jnp.dot(h_one, full_qkv, preferred_element_type=jnp.float32)
    cosine, sine_table = rope_tables(lax.axis_index("ctx") * token_rows, token_rows, HEAD_DIM)
    query_rot = rotate(as_heads(projected[:, :D]), cosine, sine_table, 1.0).astype(jnp.bfloat16)
    key_flat = (
        rotate(as_heads(projected[:, D : 2 * D]), cosine, sine_table, 1.0)
        .astype(jnp.bfloat16)
        .reshape(token_rows, D)
    )
    value_flat = projected[:, 2 * D :].astype(jnp.bfloat16)
    key_rot = as_heads(key_flat)
    value_rows = as_heads(value_flat)
    zero_heads = jnp.zeros((token_rows, HEADS, HEAD_DIM), jnp.float32)
    piece_rows = (
        lax.all_gather(key_flat, "ctx", axis=0, tiled=True),
        lax.all_gather(value_flat, "ctx", axis=0, tiled=True),
    )
    row_peak = jnp.full((HEADS, token_rows), -jnp.inf, jnp.float32)
    row_total = jnp.zeros((HEADS, token_rows), jnp.float32)
    key_piece = as_heads(piece_rows[0])
    value_piece = as_heads(piece_rows[1])
    scores = (
        jnp.einsum("qhd,khd->hqk", query_rot, key_piece, preferred_element_type=jnp.float32)
        * score_scale
    )
    new_peak = jnp.max(scores, axis=-1)
    row_fade = jnp.exp(row_peak - new_peak)
    probabilities = jnp.exp(scores - new_peak[..., None])
    new_total = row_total * row_fade + jnp.sum(probabilities, axis=-1)
    new_mixture = zero_heads * jnp.transpose(row_fade)[:, :, None] + jnp.einsum(
        "hqk,khd->qhd",
        probabilities.astype(jnp.bfloat16),
        value_piece,
        preferred_element_type=jnp.float32,
    )
    log_total = new_peak + jnp.log(new_total)
    attended = (
        (new_mixture / jnp.transpose(new_total)[:, :, None])
        .reshape(token_rows, D)
        .astype(jnp.bfloat16)
    )
    residual_stream = input_tokens + jnp.dot(
        attended, full_proj, preferred_element_type=jnp.float32
    )
    second_normed_rows, second_centered_rows, second_inverse_deviation = apply_layer_norm(
        residual_stream, second_norm_gain
    )
    h_two = second_normed_rows.astype(jnp.bfloat16)
    inner_all = jnp.dot(h_two, full_inner, preferred_element_type=jnp.float32)
    act_half = inner_all[:, :FF]
    gate_half = inner_all[:, FF:]
    activated, gelu_slope = gelu_parts(act_half)
    middle = (activated * gate_half).astype(jnp.bfloat16)
    output_rows = residual_stream + jnp.einsum(
        "tf,df->td", middle, full_down, preferred_element_type=jnp.float32
    )
    back_qkv, back_proj, back_inner, back_down = (full_qkv, full_proj, full_inner, full_down)
    upstream = cotangent[0]
    d_middle = jnp.dot(upstream, back_down, preferred_element_type=jnp.float32)
    d_inner = jnp.concatenate(
        [d_middle * gate_half * gelu_slope, d_middle * activated], axis=-1
    ).astype(jnp.bfloat16)
    second_hidden_gradient = jnp.einsum(
        "te,de->td", d_inner, back_inner, preferred_element_type=jnp.float32
    )
    residual_norm_gradient, second_gain_portion = layer_norm_gradient(
        second_hidden_gradient, second_norm_gain, second_centered_rows, second_inverse_deviation
    )
    d_resid = upstream.astype(jnp.float32) + residual_norm_gradient
    d_resid_low = d_resid.astype(jnp.bfloat16)
    d_attended = jnp.einsum(
        "td,ed->te", d_resid_low, back_proj, preferred_element_type=jnp.float32
    ).astype(jnp.bfloat16)
    grad_heads = as_heads(d_attended)
    row_delta = jnp.transpose(
        jnp.sum(grad_heads.astype(jnp.float32) * as_heads(attended).astype(jnp.float32), axis=-1)
    )
    log_whole, delta_whole = (
        lax.all_gather(log_total, "ctx", axis=1, tiled=True),
        lax.all_gather(row_delta, "ctx", axis=1, tiled=True),
    )
    piece_rows = (
        lax.all_gather(key_flat, "ctx", axis=0, tiled=True),
        lax.all_gather(value_flat, "ctx", axis=0, tiled=True),
    )
    key_part = as_heads(piece_rows[0])
    value_part = as_heads(piece_rows[1])
    probs_low, dscore = pair_terms(
        query_rot, grad_heads, log_total, row_delta, key_part, value_part, score_scale
    )
    query_grad = (
        jnp.einsum("hqk,khd->qhd", dscore, key_part, preferred_element_type=jnp.float32)
        * score_scale
    )
    piece_rows = (
        lax.all_gather(query_rot.reshape(token_rows, D), "ctx", axis=0, tiled=True),
        lax.all_gather(d_attended, "ctx", axis=0, tiled=True),
    )
    query_part = as_heads(piece_rows[0])
    grad_part = as_heads(piece_rows[1])
    probs_low, dscore = pair_terms(
        query_part, grad_part, log_whole, delta_whole, key_rot, value_rows, score_scale
    )
    key_sum = (
        jnp.einsum("hqk,qhd->khd", dscore, query_part, preferred_element_type=jnp.float32)
        * score_scale
    )
    value_sum = jnp.einsum("hqk,qhd->khd", probs_low, grad_part, preferred_element_type=jnp.float32)
    d_query = rotate(query_grad, cosine, sine_table, -1.0)
    d_key = rotate(key_sum, cosine, sine_table, -1.0)
    d_projected = jnp.concatenate(
        [
            d_query.reshape(token_rows, D),
            d_key.reshape(token_rows, D),
            value_sum.reshape(token_rows, D),
        ],
        axis=-1,
    ).astype(jnp.bfloat16)
    first_hidden_gradient = jnp.einsum(
        "te,de->td", d_projected, back_qkv, preferred_element_type=jnp.float32
    )
    input_norm_gradient, first_gain_portion = layer_norm_gradient(
        first_hidden_gradient, first_norm_gain, first_centered_rows, first_inverse_deviation
    )
    input_grad = d_resid + input_norm_gradient

    def grad_rows(start, count):
        return jnp.concatenate(
            [
                jnp.einsum("td,te->de", h_one, d_projected, preferred_element_type=jnp.float32),
                jnp.einsum("te,td->ed", attended, d_resid_low, preferred_element_type=jnp.float32),
                jnp.einsum("td,te->de", h_two, d_inner, preferred_element_type=jnp.float32),
                jnp.einsum("td,tf->df", upstream, middle, preferred_element_type=jnp.float32),
                first_gain_portion[:, None],
                second_gain_portion[:, None],
            ],
            axis=1,
        )

    owned_rows = D // lax.axis_size(("batch", "ctx"))
    grad_share = lax.psum_scatter(
        grad_rows(jnp.int32(0), owned_rows * lax.axis_size(("batch", "ctx"))),
        ("batch", "ctx"),
        scatter_dimension=0,
        tiled=True,
    )
    qkv_share = grad_share[:, : 3 * D]
    proj_share = grad_share[:, 3 * D : 4 * D]
    inner_share = grad_share[:, 4 * D : 4 * D + 2 * FF]
    down_share = grad_share[:, 4 * D + 2 * FF : 4 * D + 3 * FF]
    first_share = grad_share[:, 4 * D + 3 * FF]
    second_share = grad_share[:, 4 * D + 3 * FF + 1]
    return (
        output_rows.astype(jnp.bfloat16)[None],
        input_grad[None],
        qkv_share,
        proj_share,
        inner_share,
        down_share,
        first_share,
        second_share,
    )


def solution(mesh):
    placed = (
        P("batch", "ctx", None),
        P("batch", "ctx", None),
        P(("batch", "ctx"), None),
        P(("batch", "ctx"), None),
        P(("batch", "ctx"), None),
        P(("batch", "ctx"), None),
        P(("batch", "ctx")),
        P(("batch", "ctx")),
    )
    return jax.shard_map(
        local,
        mesh=mesh,
        in_specs=placed,
        out_specs=(
            P("batch", "ctx", None),
            P("batch", "ctx", None),
            P(("batch", "ctx"), None),
            P(("batch", "ctx"), None),
            P(("batch", "ctx"), None),
            P(("batch", "ctx"), None),
            P(("batch", "ctx")),
            P(("batch", "ctx")),
        ),
        check_vma=False,
    )
```

profile of v0, /device:TPU:0, one launch (start us, length us, event | category | flops | bytes accessed | tf_op | source)
XLA Modules:
  0.0 641.2 jit_solution(14519602445404281982)
XLA Ops:
  8.0 0.8 dynamic-update-slice
  8.8 0.8 dynamic-update-slice.1
  9.6 42.2 %all-reduce.2 = (bf16[768]{0:T(1024)(128)(2,1)S(1)}, bf16[768]{0:T(1024)(128)(2,1)S(1)}) all-reduce(bf16[768]{0:T(1024)(128)(2,1)S(1)} %dynamic-update-slice, bf16[768]{0:T(1024)(128)(2,1)S(1)} %dynamic-update-slice.1), channel_id=1, replica_groups=mesh['batch'=4,'ctx'=8] {'batch','ctx'}, use_global_device_ids=true, to_apply=%add | all-reduce | flops 1536 | bytes 6144
  51.9 1.0 convert_reduce_fusion
  52.9 1.1 fusion.58
  54.1 0.8 broadcast_multiply_fusion
  54.8 19.1 %all-gather.9.cloned.1.call-done = bf16[768,2304]{1,0:T(8,128)(2,1)} async-done(((bf16[24,2304]{1,0:T(8,128)(2,1)}), bf16[768,2304]{1,0:T(8,128)(2,1)}) %all-gather.9.cloned.1.call-update) | async-done | bytes 3538960 | tf_op jit(solution)/shard_map/all_gather | solution.py:83
  73.9 2.8 fusion.79
  82.0 22.7 %all-gather.11.cloned.1.call-done = bf16[1024,768]{0,1:T(8,128)(2,1)} async-done(((bf16[128,768]{0,1:T(8,128)(2,1)}), bf16[1024,768]{0,1:T(8,128)(2,1)}) %all-gather.11.cloned.1.call-update) | async-done | bytes 1572880 | tf_op jit(solution)/shard_map/all_gather | solution.py:110
  104.7 2.5 multiply_reduce_fusion
  107.2 1.3 fusion
  108.5 1.4 copy-done
  109.9 21.1 %all-gather.13.cloned.1.call-done = bf16[1024,768]{1,0:T(8,128)(2,1)} async-done(((bf16[128,768]{1,0:T(8,128)(2,1)}), bf16[1024,768]{1,0:T(8,128)(2,1)}) %all-gather.13.cloned.1.call-update) | async-done | bytes 1572880 | tf_op jit(solution)/shard_map/all_gather | solution.py:111
  131.0 1.7 copy.27
  132.7 4.8 fusion.35
  137.5 49.6 %all-gather.15.cloned.1.call-done = bf16[768,768]{1,0:T(8,128)(2,1)} async-done(((bf16[24,768]{1,0:T(8,128)(2,1)}), bf16[768,768]{1,0:T(8,128)(2,1)}) %all-gather.15.cloned.1.call-update) | async-done | bytes 1179664 | tf_op jit(solution)/shard_map/all_gather | solution.py:84
  187.1 1.7 fusion.84
  189.1 59.9 %all-gather.17.cloned.1.call-done = bf16[768,2304]{1,0:T(8,128)(2,1)} async-done(((bf16[24,2304]{1,0:T(8,128)(2,1)}), bf16[768,2304]{1,0:T(8,128)(2,1)}) %all-gather.17.cloned.1.call-update) | async-done | bytes 3538960 | tf_op jit(solution)/shard_map/all_gather | solution.py:85
  249.0 2.7 fusion.81
  251.6 54.4 %all-gather.19.cloned.1.call-done = bf16[768,1152]{1,0:T(8,128)(2,1)} async-done(((bf16[24,1152]{1,0:T(8,128)(2,1)}), bf16[768,1152]{1,0:T(8,128)(2,1)}) %all-gather.19.cloned.1.call-update) | async-done | bytes 1769488 | tf_op jit(solution)/shard_map/all_gather | solution.py:86
  306.1 2.2 fusion.43
  308.6 1.4 multiply_reduce_fusion.1
  310.3 1.2 convolution_convert_fusion
  311.6 0.8 copy.30
  312.4 1.1 copy.28
  313.5 0.9 broadcast_in_dim.19
  314.4 15.1 %all_gather.47 = f32[12,1024]{1,0:T(8,128)} all-gather(f32[12,128]{1,0:T(8,128)S(1)} %get-tuple-element.36), channel_id=1, replica_groups=mesh['batch'=4,'ctx'=8] {'ctx'}, dimensions={1}, use_global_device_ids=true | all-gather | bytes 55296 | tf_op jit(solution)/shard_map/all_gather | solution.py:174
  329.6 15.2 %all_gather.49 = f32[12,1024]{1,0:T(8,128)} all-gather(f32[12,128]{1,0:T(8,128)S(1)} %bitcast.128), channel_id=1, replica_groups=mesh['batch'=4,'ctx'=8] {'ctx'}, dimensions={1}, use_global_device_ids=true | all-gather | bytes 55296 | tf_op jit(solution)/shard_map/all_gather | solution.py:175
  345.3 3.8 convolution_bitcast_fusion
  349.1 4.1 fusion.59
  353.2 5.1 fusion.85
  358.4 7.3 %fusion.23 = f32[128,12,64]{0,2,1:T(8,128)} fusion(bf16[1024,12,64]{0,2,1:T(8,128)(2,1)} %bitcast.114, f32[12,128,1024]{2,1,0:T(8,128)} %copy-done, f32[12,128]{1,0:T(8,128)S(1)} %bitcast.129, f32[12,128]{1,0:T(8,128)} %copy-done.21, bf16[128,12,64]{0,2,1:T(8,128)(2,1)} %bitcast.120, bf16[1024,12,64]{0,2,1:T(8,128)(2,1)} %bitcast.110), kind=kOutput, calls=%fused_computation.25 | convolution fusion | flops 410615808 | bytes 10039296 | tf_op jit(solution)/shard_map/hqk,khd->qhd/dot_general | solution.py:187
  365.6 2.6 copy.29
  368.2 4.5 fusion.28
  372.7 8.9 %fusion.21 = f32[128,12,64]{0,2,1:T(8,128)} fusion(bf16[1024,12,64]{0,2,1:T(8,128)(2,1)} %bitcast.116, f32[12,1024,128]{2,1,0:T(8,128)} %fusion.85, f32[12,1024]{1,0:T(8,128)} %all_gather.49, f32[12,1024]{1,0:T(8,128)} %all_gather.47, bf16[1024,12,64]{0,2,1:T(8,128)(2,1)} %bitcast.106, bf16[128,12,64]{0,2,1:T(8,128)(2,1)} %bitcast.127), kind=kOutput, calls=%fused_computation.23 | convolution fusion | flops 410615808 | bytes 10125312 | tf_op jit(solution)/shard_map/hqk,qhd->khd/dot_general | solution.py:200
  381.6 1.4 subtract_convert_fusion.1
  383.0 4.1 fusion.61
  387.1 2.6 fusion.57
  389.7 0.9 broadcast_in_dim.18
  390.6 22.2 %concatenate.31 = f32[768,6530]{1,0:T(8,128)} concatenate(f32[768,2304]{1,0:T(8,128)} %fusion.61, f32[768,768]{1,0:T(8,128)S(1)} %fusion.66, f32[768,2304]{1,0:T(8,128)} %fusion.59, f32[768,1152]{1,0:T(8,128)} %convolution_bitcast_fusion, f32[768,1]{1,0:T(8,128)} %broadcast_in_dim.18, f32[768,1]{1,0:T(8,128)} %broadcast_in_dim.19), dimensions={1} | concatenate | bytes 40120320 | tf_op jit(solution)/shard_map/concatenate | solution.py:223
  412.9 1.2 copy-done.4
  414.1 2.9 fusion.31
  417.0 0.9 fusion.56
  417.9 210.3 %reduce-scatter.2.cloned.1.call-done = f32[24,6530]{1,0:T(8,128)} async-done(((f32[768,6530]{1,0:T(8,128)}), f32[24,6530]{1,0:T(8,128)}) %reduce-scatter.2.cloned.1.call-update) | async-done | bytes 626896 | tf_op jit(solution)/shard_map/reduce_scatter | solution.py:236
  628.3 1.5 slice_reduce_fusion
  629.7 1.5 slice.91
  631.3 1.5 slice.93
  632.8 1.8 fusion.83
  (108 shorter events, 7.3 us)
Async XLA Ops:
  7.2 66.8 %all-gather.9.cloned.1.call-start = ((), (), s32[]{:S(2)}) async-start(), calls=%async_computation.1 | async-start | bytes 3649536 | tf_op jit(solution)/shard_map/all_gather | solution.py:83
  7.9 96.8 %all-gather.11.cloned.1.call-start = ((), (), s32[]{:S(2)}) async-start(), calls=%async_computation.2 | async-start | bytes 1769472 | tf_op jit(solution)/shard_map/all_gather | solution.py:110
  52.9 23.9 %copy-start.22 = (f32[128]{0:T(128)}, f32[128]{0:T(128)S(1)}, u32[]{:S(2)}) copy-start(f32[128]{0:T(128)S(1)} %broadcast_multiply_fusion.6) | copy-start | bytes 1540
  54.1 22.7 %copy-start.26 = (f32[128]{0:T(128)}, f32[128]{0:T(128)S(1)}, u32[]{:S(2)}) copy-start(f32[128]{0:T(128)S(1)} %add_rsqrt_fusion.1) | copy-start | bytes 1540
  54.8 22.3 %copy-start.20 = (f32[128,32]{0,1:T(8,128)}, f32[128,32]{0,1:T(8,128)S(1)}, u32[]{:S(2)}) copy-start(f32[128,32]{0,1:T(8,128)S(1)} %get-tuple-element.40) | copy-start | bytes 49156
  77.3 0.6 copy-start.9
  77.3 1.3 copy-start.11
  78.6 52.3 %all-gather.13.cloned.1.call-start = ((), (), s32[]{:S(2)}) async-start(), calls=%async_computation.3 | async-start | bytes 1769472 | tf_op jit(solution)/shard_map/all_gather | solution.py:111
  79.4 107.7 %all-gather.15.cloned.1.call-start = ((), (), s32[]{:S(2)}) async-start(), calls=%async_computation.4 | async-start | bytes 1216512 | tf_op jit(solution)/shard_map/all_gather | solution.py:84
  80.0 169.0 %all-gather.17.cloned.1.call-start = ((), (), s32[]{:S(2)}) async-start(), calls=%async_computation.5 | async-start | bytes 3649536 | tf_op jit(solution)/shard_map/all_gather | solution.py:85
  80.6 225.5 %all-gather.19.cloned.1.call-start = ((), (), s32[]{:S(2)}) async-start(), calls=%async_computation.6 | async-start | bytes 1824768 | tf_op jit(solution)/shard_map/all_gather | solution.py:86
  81.2 272.1 %all-gather.21.cloned.1.call-start = ((), (), s32[]{:S(2)}) async-start(), calls=%async_computation.7 | async-start | bytes 1769472 | tf_op jit(solution)/shard_map/all_gather | solution.py:191
  81.9 283.7 %all-gather.23.cloned.1.call-start = ((), (), s32[]{:S(2)}) async-start(), calls=%async_computation.8 | async-start | bytes 1769472 | tf_op jit(solution)/shard_map/all_gather | solution.py:192
  107.2 2.7 copy-start
  109.9 204.6 %copy-start.21 = (f32[12,128]{1,0:T(8,128)}, f32[12,128]{1,0:T(8,128)S(1)}, u32[]{:S(2)}) copy-start(f32[12,128]{1,0:T(8,128)S(1)} %get-tuple-element.36) | copy-start | bytes 18436
  132.7 4.8 copy-start.8
  132.7 54.4 %copy-start.1 = (bf16[1,128,768]{2,1,0:T(8,128)(2,1)S(1)}, bf16[1,128,768]{2,1,0:T(8,128)(2,1)}, u32[]{:S(2)}) copy-start(bf16[1,128,768]{2,1,0:T(8,128)(2,1)} %param.8) | copy-start | bytes 589828
  188.9 117.2 %copy-start.13 = (bf16[1,128,768]{2,1,0:T(8,128)(2,1)S(1)}, bf16[1,128,768]{2,1,0:T(8,128)(2,1)}, u32[]{:S(2)}) copy-start(bf16[1,128,768]{2,1,0:T(8,128)(2,1)} %param.9) | copy-start | bytes 589828
  188.9 121.2 %copy-start.24 = (f32[128]{0:T(128)}, f32[128]{0:T(128)S(1)}, u32[]{:S(2)}) copy-start(f32[128]{0:T(128)S(1)} %broadcast_multiply_fusion.5) | copy-start | bytes 1540
  189.1 121.0 %copy-start.28 = (f32[128]{0:T(128)}, f32[128]{0:T(128)S(1)}, u32[]{:S(2)}) copy-start(f32[128]{0:T(128)S(1)} %add_rsqrt_fusion) | copy-start | bytes 1540
  251.6 56.7 %copy-start.3 = (f32[128,2304]{1,0:T(8,128)}, f32[128,2304]{1,0:T(8,128)S(1)}, u32[]{:S(2)}) copy-start(f32[128,2304]{1,0:T(8,128)S(1)} %fusion.81) | copy-start | bytes 3538948
  306.1 2.5 copy-start.5
  308.3 1.7 copy-start.18
  308.3 2.0 copy-start.16
  308.6 1.7 copy-start.2
  308.6 3.0 copy-start.7
  311.5 316.7 %reduce-scatter.2.cloned.1.call-start = ((), (), s32[]{:S(2)}) async-start(), calls=%async_computation.9 | async-start | bytes 21086208 | tf_op jit(solution)/shard_map/reduce_scatter | solution.py:236
  313.5 16.1 %copy-start.14 = (bf16[128,768]{0,1:T(8,128)(2,1)}, bf16[128,768]{0,1:T(8,128)(2,1)S(1)}, u32[]{:S(2)}) copy-start(bf16[128,768]{0,1:T(8,128)(2,1)S(1)} %copy.28) | copy-start | bytes 589828
  344.8 4.2 copy-start.17
  344.8 4.2 copy-start.19
  344.8 4.2 copy-start.25
  344.8 4.2 copy-start.29
  349.1 4.2 copy-start.10
  349.1 4.1 copy-start.12
  372.7 10.3 %copy-start.23 = (f32[128]{0:T(128)S(1)}, f32[128]{0:T(128)}, u32[]{:S(2)}) copy-start(f32[128]{0:T(128)} %copy-done.22) | copy-start | bytes 1540
  372.7 10.3 %copy-start.27 = (f32[128]{0:T(128)S(1)}, f32[128]{0:T(128)}, u32[]{:S(2)}) copy-start(f32[128]{0:T(128)} %copy-done.26) | copy-start | bytes 1540
  383.0 4.1 copy-start.6
  412.8 1.3 copy-start.4
  412.8 4.2 copy-start.30
  414.1 2.9 copy-start.15
Sparse Core Ops, SparseCore 0:
  11.0 62.9 all-gather.8
  78.8 25.8 all-gather.10
  106.9 24.0 all-gather.12
  133.9 53.2 all-gather.14
  190.0 58.9 all-gather.16
  251.7 54.3 all-gather.18
  308.2 26.2 all-gather.20
  336.8 24.9 all-gather.22
  413.0 215.2 reduce-scatter.1
where the time goes:
time: 642 us; the launch traced here: 641 us
  waiting for transfers between devices  439 us (68%)
  blocking collectives  72.5 us (11%)
  matrix products  62.9 us (10%)
  local copies, waits for them, and re-layouts  43 us (7%)
  between operations  14.3 us (2%)
  other arithmetic  8.55 us (1%)
    reduce_scatter x1, waiting for transfers between devices, local(): lax.psum_scatter(grad_rows(jnp.int32(0), owned_rows * lax.axis_size(('bat...  210 us
    all_gather x1, waiting for transfers between devices, local(): lax.all_gather(w_inner, ('batch', 'ctx'), axis=0, tiled=True)  59.9 us
    all_gather x1, waiting for transfers between devices, local(): lax.all_gather(w_down, ('batch', 'ctx'), axis=0, tiled=True)  54.4 us
    all_gather x1, waiting for transfers between devices, local(): lax.all_gather(w_proj, ('batch', 'ctx'), axis=0, tiled=True)  49.6 us
    unnamed x1, blocking collectives  42.2 us
    all_gather x1, waiting for transfers between devices, local(): lax.all_gather(key_flat, 'ctx', axis=0, tiled=True)  22.7 us
    concatenate x1, local copies, waits for them, and re-layouts, grad_rows(): jnp.concatenate([jnp.einsum('td,te->de', h_one, d_projected, preferred_el...  22.2 us
    all_gather x1, waiting for transfers between devices, local(): lax.all_gather(value_flat, 'ctx', axis=0, tiled=True)  21.1 us
  transfers between devices with their start and end apart: 9, of which 7 were waited for; matrix products, arithmetic and copies ran while one was open for 8% of the time, Pallas kernels for 0%

commit v1 on v0

--- a/solution.py
+++ b/solution.py
@@ -9,6 +9,12 @@
 FF = 1152
 norm_eps = 1e-05
 rope_base = 160000.0
+
+
+def gather_from_all(x, axis, dim):
+    devices = lax.axis_size(axis)
+    repeats = [devices if d == dim else 1 for d in range(x.ndim)]
+    return lax.all_to_all(jnp.tile(x, repeats), axis, split_axis=dim, concat_axis=dim, tiled=True)
 
 
 def apply_layer_norm(values, gain_vector):
@@ -82,7 +88,7 @@
     full_qkv, full_proj, full_inner, full_down, gain_first, gain_second = (
         lax.all_gather(w_qkv, ("batch", "ctx"), axis=0, tiled=True),
         lax.all_gather(w_proj, ("batch", "ctx"), axis=0, tiled=True),
-        lax.all_gather(w_inner, ("batch", "ctx"), axis=0, tiled=True),
+        gather_from_all(w_inner, ("batch", "ctx"), 0),
         lax.all_gather(w_down, ("batch", "ctx"), axis=0, tiled=True),
         lax.all_gather(norm1_gain, ("batch", "ctx"), axis=0, tiled=True),
         lax.all_gather(norm2_gain, ("batch", "ctx"), axis=0, tiled=True),

time: 642 us -> 619 us (0.964)
  waiting for transfers between devices: 439 us -> 411 us
    all_gather x1 -> x0, waiting for transfers between devices: 59.9 us -> none  [local(): lax.all_gather(w_inner, ('batch', 'ctx'), axis=0, tiled=True)]
    all_gather x1, waiting for transfers between devices: 22.7 us -> 53 us  [local(): lax.all_gather(key_flat, 'ctx', axis=0, tiled=True)]
  transfers between devices with their start and end apart: 9 -> 9, of which waited for: 7 -> 6; matrix products, arithmetic and copies ran while one was open for 8% -> 9% of each run, Pallas kernels for 0% -> 0%
where the time goes in v1:
time: 619 us; the launch traced here: 618 us
  waiting for transfers between devices  411 us (66%)
  blocking collectives  72.8 us (12%)
  matrix products  61.7 us (10%)
  local copies, waits for them, and re-layouts  44.7 us (7%)
  between operations  14.7 us (2%)
  other arithmetic  8.55 us (1%)
    reduce_scatter x1, waiting for transfers between devices, local(): lax.psum_scatter(grad_rows(jnp.int32(0), owned_rows * lax.axis_size(('bat...  210 us
    all_gather x1, waiting for transfers between devices, local(): lax.all_gather(key_flat, 'ctx', axis=0, tiled=True)  53 us
    all_gather x1, waiting for transfers between devices, local(): lax.all_gather(w_down, ('batch', 'ctx'), axis=0, tiled=True)  52.6 us
    all_gather x1, waiting for transfers between devices, local(): lax.all_gather(w_proj, ('batch', 'ctx'), axis=0, tiled=True)  48.5 us
    unnamed x1, blocking collectives  42.2 us
    all_gather x1, waiting for transfers between devices, local(): lax.all_gather(value_flat, 'ctx', axis=0, tiled=True)  25.6 us
    concatenate x1, local copies, waits for them, and re-layouts, grad_rows(): jnp.concatenate([jnp.einsum('td,te->de', h_one, d_projected, preferred_el...  22.2 us
    all_gather x1, waiting for transfers between devices, local(): lax.all_gather(w_qkv, ('batch', 'ctx'), axis=0, tiled=True)  19.8 us
  transfers between devices with their start and end apart: 9, of which 6 were waited for; matrix products, arithmetic and copies ran while one was open for 9% of the time, Pallas kernels for 0%

profile of v1, /device:TPU:0, one launch (start us, length us, event | category | flops | bytes accessed | tf_op | source)
XLA Modules:
  0.0 617.6 jit_solution(5800443226296703146)
XLA Ops:
  8.0 0.8 dynamic-update-slice
  8.8 0.8 dynamic-update-slice.1
  9.7 42.2 %all-reduce.2 = (bf16[768]{0:T(1024)(128)(2,1)S(1)}, bf16[768]{0:T(1024)(128)(2,1)S(1)}) all-reduce(bf16[768]{0:T(1024)(128)(2,1)S(1)} %dynamic-update-slice, bf16[768]{0:T(1024)(128)(2,1)S(1)} %dynamic-update-slice.1), channel_id=1, replica_groups=mesh['batch'=4,'ctx'=8] {'batch','ctx'}, use_global_device_ids=true, to_apply=%add | all-reduce | flops 1536 | bytes 6144
  51.9 1.0 convert_reduce_fusion
  53.0 1.1 fusion.58
  54.1 19.8 %all-gather.8.cloned.1.call-done = bf16[768,2304]{1,0:T(8,128)(2,1)} async-done(((bf16[24,2304]{1,0:T(8,128)(2,1)}), bf16[768,2304]{1,0:T(8,128)(2,1)}) %all-gather.8.cloned.1.call-update) | async-done | bytes 3538960 | tf_op jit(solution)/shard_map/all_gather | solution.py:89
  73.9 2.8 fusion.79
  80.7 2.0 tile.2
  82.7 3.6 all-to-all-start
  87.7 25.6 %all-gather.12.cloned.1.call-done = bf16[1024,768]{1,0:T(8,128)(2,1)} async-done(((bf16[128,768]{1,0:T(8,128)(2,1)}), bf16[1024,768]{1,0:T(8,128)(2,1)}) %all-gather.12.cloned.1.call-update) | async-done | bytes 1572880 | tf_op jit(solution)/shard_map/all_gather | solution.py:117
  113.3 1.7 copy.27
  115.0 53.0 %all-gather.10.cloned.1.call-done = bf16[1024,768]{0,1:T(8,128)(2,1)} async-done(((bf16[128,768]{0,1:T(8,128)(2,1)}), bf16[1024,768]{0,1:T(8,128)(2,1)}) %all-gather.10.cloned.1.call-update) | async-done | bytes 1572880 | tf_op jit(solution)/shard_map/all_gather | solution.py:116
  168.0 2.5 multiply_reduce_fusion
  170.5 1.3 fusion
  171.9 1.3 copy-done
  173.2 1.5 fusion.35
  174.6 48.5 %all-gather.14.cloned.1.call-done = bf16[768,768]{1,0:T(8,128)(2,1)} async-done(((bf16[24,768]{1,0:T(8,128)(2,1)}), bf16[768,768]{1,0:T(8,128)(2,1)}) %all-gather.14.cloned.1.call-update) | async-done | bytes 1179664 | tf_op jit(solution)/shard_map/all_gather | solution.py:90
  223.2 1.7 fusion.84
  225.1 2.7 fusion.81
  227.8 52.6 %all-gather.16.cloned.1.call-done = bf16[768,1152]{1,0:T(8,128)(2,1)} async-done(((bf16[24,1152]{1,0:T(8,128)(2,1)}), bf16[768,1152]{1,0:T(8,128)(2,1)}) %all-gather.16.cloned.1.call-update) | async-done | bytes 1769488 | tf_op jit(solution)/shard_map/all_gather | solution.py:92
  280.4 2.1 fusion.43
  282.5 3.6 multiply_reduce_fusion.1
  286.4 1.2 convolution_convert_fusion
  287.7 0.8 copy.30
  288.5 1.1 copy.28
  289.6 0.9 broadcast_in_dim.19
  290.5 15.3 %all_gather.43 = f32[12,1024]{1,0:T(8,128)} all-gather(f32[12,128]{1,0:T(8,128)S(1)} %get-tuple-element.36), channel_id=1, replica_groups=mesh['batch'=4,'ctx'=8] {'ctx'}, dimensions={1}, use_global_device_ids=true | all-gather | bytes 55296 | tf_op jit(solution)/shard_map/all_gather | solution.py:180
  305.9 15.2 %all_gather.45 = f32[12,1024]{1,0:T(8,128)} all-gather(f32[12,128]{1,0:T(8,128)S(1)} %bitcast.129), channel_id=1, replica_groups=mesh['batch'=4,'ctx'=8] {'ctx'}, dimensions={1}, use_global_device_ids=true | all-gather | bytes 55296 | tf_op jit(solution)/shard_map/all_gather | solution.py:181
  321.6 3.8 convolution_bitcast_fusion
  325.4 4.1 fusion.59
  329.6 5.1 fusion.85
  334.7 7.3 %fusion.23 = f32[128,12,64]{0,2,1:T(8,128)} fusion(bf16[1024,12,64]{0,2,1:T(8,128)(2,1)} %bitcast.115, f32[12,128,1024]{2,1,0:T(8,128)} %copy-done, f32[12,128]{1,0:T(8,128)S(1)} %bitcast.130, f32[12,128]{1,0:T(8,128)} %copy-done.21, bf16[128,12,64]{0,2,1:T(8,128)(2,1)} %bitcast.121, bf16[1024,12,64]{0,2,1:T(8,128)(2,1)} %bitcast.111), kind=kOutput, calls=%fused_computation.25 | convolution fusion | flops 410615808 | bytes 10039296 | tf_op jit(solution)/shard_map/hqk,khd->qhd/dot_general | solution.py:193
  341.9 2.6 copy.29
  344.5 4.5 fusion.28
  349.0 8.9 %fusion.21 = f32[128,12,64]{0,2,1:T(8,128)} fusion(bf16[1024,12,64]{0,2,1:T(8,128)(2,1)} %bitcast.117, f32[12,1024,128]{2,1,0:T(8,128)} %fusion.85, f32[12,1024]{1,0:T(8,128)} %all_gather.45, f32[12,1024]{1,0:T(8,128)} %all_gather.43, bf16[1024,12,64]{0,2,1:T(8,128)(2,1)} %bitcast.107, bf16[128,12,64]{0,2,1:T(8,128)(2,1)} %bitcast.128), kind=kOutput, calls=%fused_computation.23 | convolution fusion | flops 410615808 | bytes 10125312 | tf_op jit(solution)/shard_map/hqk,qhd->khd/dot_general | solution.py:206
  357.9 1.4 subtract_convert_fusion.1
  359.3 4.1 fusion.61
  363.4 2.6 fusion.57
  366.0 0.9 broadcast_in_dim.18
  367.0 22.2 %concatenate.31 = f32[768,6530]{1,0:T(8,128)} concatenate(f32[768,2304]{1,0:T(8,128)} %fusion.61, f32[768,768]{1,0:T(8,128)S(1)} %fusion.66, f32[768,2304]{1,0:T(8,128)} %fusion.59, f32[768,1152]{1,0:T(8,128)} %convolution_bitcast_fusion, f32[768,1]{1,0:T(8,128)} %broadcast_in_dim.18, f32[768,1]{1,0:T(8,128)} %broadcast_in_dim.19), dimensions={1} | concatenate | bytes 40120320 | tf_op jit(solution)/shard_map/concatenate | solution.py:229
  389.2 1.2 copy-done.4
  390.5 2.9 fusion.31
  393.4 0.9 fusion.56
  394.3 210.1 %reduce-scatter.2.cloned.1.call-done = f32[24,6530]{1,0:T(8,128)} async-done(((f32[768,6530]{1,0:T(8,128)}), f32[24,6530]{1,0:T(8,128)}) %reduce-scatter.2.cloned.1.call-update) | async-done | bytes 626896 | tf_op jit(solution)/shard_map/reduce_scatter | solution.py:242
  604.4 1.5 slice_reduce_fusion
  605.9 1.5 slice.91
  607.4 1.5 slice.93
  608.9 1.8 fusion.83
  (108 shorter events, 7.2 us)
Async XLA Ops:
  7.2 66.7 %all-gather.8.cloned.1.call-start = ((), (), s32[]{:S(2)}) async-start(), calls=%async_computation.2 | async-start | bytes 3649536 | tf_op jit(solution)/shard_map/all_gather | solution.py:89
  7.9 105.4 %all-gather.12.cloned.1.call-start = ((), (), s32[]{:S(2)}) async-start(), calls=%async_computation.4 | async-start | bytes 1769472 | tf_op jit(solution)/shard_map/all_gather | solution.py:117
  52.9 24.6 %copy-start.22 = (f32[128]{0:T(128)}, f32[128]{0:T(128)S(1)}, u32[]{:S(2)}) copy-start(f32[128]{0:T(128)S(1)} %broadcast_multiply_fusion.6) | copy-start | bytes 1540
  54.1 23.4 %copy-start.26 = (f32[128]{0:T(128)}, f32[128]{0:T(128)S(1)}, u32[]{:S(2)}) copy-start(f32[128]{0:T(128)S(1)} %add_rsqrt_fusion.1) | copy-start | bytes 1540
  76.7 4.0 copy-start.20
  77.4 90.6 %all-gather.10.cloned.1.call-start = ((), (), s32[]{:S(2)}) async-start(), calls=%async_computation.3 | async-start | bytes 1769472 | tf_op jit(solution)/shard_map/all_gather | solution.py:116
  78.3 4.4 copy-start.19
  78.8 0.6 copy-start.8
  78.8 1.3 copy-start.10
  80.1 143.0 %all-gather.14.cloned.1.call-start = ((), (), s32[]{:S(2)}) async-start(), calls=%async_computation.5 | async-start | bytes 1216512 | tf_op jit(solution)/shard_map/all_gather | solution.py:90
  82.7 142.4 %all-to-all-start = ((bf16[32,24,2304]{2,1,0:T(8,128)(2,1)}), bf16[32,24,2304]{2,1,0:T(8,128)(2,1)}, u32[]{:S(2)}, u32[]{:S(2)}) async-start(bf16[32,24,2304]{2,1,0:T(8,128)(2,1)} %tile.2), calls=%async_computation | async-start | bytes 7077888 | tf_op jit(solution)/shard_map/all_to_all | solution.py:17
  86.3 194.1 %all-gather.16.cloned.1.call-start = ((), (), s32[]{:S(2)}) async-start(), calls=%async_computation.6 | async-start | bytes 1824768 | tf_op jit(solution)/shard_map/all_gather | solution.py:92
  86.9 242.7 %all-gather.18.cloned.1.call-start = ((), (), s32[]{:S(2)}) async-start(), calls=%async_computation.7 | async-start | bytes 1769472 | tf_op jit(solution)/shard_map/all_gather | solution.py:197
  87.6 254.3 %all-gather.20.cloned.1.call-start = ((), (), s32[]{:S(2)}) async-start(), calls=%async_computation.8 | async-start | bytes 1769472 | tf_op jit(solution)/shard_map/all_gather | solution.py:198
  115.0 56.8 %copy-start.7 = (bf16[1024,768]{0,1:T(8,128)(2,1)}, bf16[1024,768]{0,1:T(8,128)(2,1)S(1)}, u32[]{:S(2)}) copy-start(bf16[1024,768]{0,1:T(8,128)(2,1)S(1)} %copy.27) | copy-start | bytes 4718596
  170.5 2.7 copy-start
  171.8 118.7 %copy-start.21 = (f32[12,128]{1,0:T(8,128)}, f32[12,128]{1,0:T(8,128)S(1)}, u32[]{:S(2)}) copy-start(f32[12,128]{1,0:T(8,128)S(1)} %get-tuple-element.36) | copy-start | bytes 18436
  173.2 50.0 %copy-start.1 = (bf16[1,128,768]{2,1,0:T(8,128)(2,1)S(1)}, bf16[1,128,768]{2,1,0:T(8,128)(2,1)}, u32[]{:S(2)}) copy-start(bf16[1,128,768]{2,1,0:T(8,128)(2,1)} %param.8) | copy-start | bytes 589828
  224.9 55.5 %copy-start.12 = (bf16[1,128,768]{2,1,0:T(8,128)(2,1)S(1)}, bf16[1,128,768]{2,1,0:T(8,128)(2,1)}, u32[]{:S(2)}) copy-start(bf16[1,128,768]{2,1,0:T(8,128)(2,1)} %param.9) | copy-start | bytes 589828
  224.9 61.3 %copy-start.24 = (f32[128]{0:T(128)}, f32[128]{0:T(128)S(1)}, u32[]{:S(2)}) copy-start(f32[128]{0:T(128)S(1)} %broadcast_multiply_fusion.5) | copy-start | bytes 1540
  225.1 61.1 %copy-start.28 = (f32[128]{0:T(128)}, f32[128]{0:T(128)S(1)}, u32[]{:S(2)}) copy-start(f32[128]{0:T(128)S(1)} %add_rsqrt_fusion) | copy-start | bytes 1540
  227.8 54.7 %copy-start.3 = (f32[128,2304]{1,0:T(8,128)}, f32[128,2304]{1,0:T(8,128)S(1)}, u32[]{:S(2)}) copy-start(f32[128,2304]{1,0:T(8,128)S(1)} %fusion.81) | copy-start | bytes 3538948
  282.5 3.7 copy-start.17
  282.5 3.9 copy-start.15
  282.5 3.9 copy-start.2
  282.5 5.2 copy-start.6
  287.6 316.7 %reduce-scatter.2.cloned.1.call-start = ((), (), s32[]{:S(2)}) async-start(), calls=%async_computation.9 | async-start | bytes 21086208 | tf_op jit(solution)/shard_map/reduce_scatter | solution.py:242
  289.6 16.3 %copy-start.13 = (bf16[128,768]{0,1:T(8,128)(2,1)}, bf16[128,768]{0,1:T(8,128)(2,1)S(1)}, u32[]{:S(2)}) copy-start(bf16[128,768]{0,1:T(8,128)(2,1)S(1)} %copy.28) | copy-start | bytes 589828
  321.1 4.2 copy-start.16
  321.1 4.2 copy-start.18
  321.1 4.2 copy-start.25
  321.1 4.2 copy-start.29
  325.4 4.2 copy-start.9
  325.4 4.2 copy-start.11
  349.0 10.3 %copy-start.23 = (f32[128]{0:T(128)S(1)}, f32[128]{0:T(128)}, u32[]{:S(2)}) copy-start(f32[128]{0:T(128)} %copy-done.22) | copy-start | bytes 1540
  349.0 10.3 %copy-start.27 = (f32[128]{0:T(128)S(1)}, f32[128]{0:T(128)}, u32[]{:S(2)}) copy-start(f32[128]{0:T(128)} %copy-done.26) | copy-start | bytes 1540
  359.3 4.1 copy-start.5
  389.2 1.3 copy-start.4
  389.2 4.2 copy-start.30
  390.5 2.9 copy-start.14
Sparse Core Ops, SparseCore 0:
  11.0 62.8 all-gather.7
  77.5 35.7 all-gather.11
  115.5 52.4 all-gather.9
  170.9 52.2 all-gather.13
  225.9 54.4 all-gather.15
  282.4 26.3 all-gather.17
  311.1 25.7 all-gather.19
  389.3 215.0 reduce-scatter.1
